TPU v7x, 256 devices: a whole 4x4x8 slice. The times are simulated.
256 devices in a mesh: users: 32 (over x, z), rb: 8 (over y, core).
Axes of the slice: x: 4, y: 4, z: 8, core: 2. Of those that a mesh axis runs over, the one named last changes fastest.
Arguments:
- channel: bfloat16 [32768, 32, 3, 128], P('users', 'rb'), may hold values from -13 to 13
- serving: int32 [32768], P('users'), may hold values from 0 to 63, as said below
- interferers: int32 [32768, 2], P('users'), may hold values from 0 to 63, as said below
- plan: int32 [64, 32, 16], P(None, 'rb'), may hold values from 0 to 32767, as said below
- regularizer: float32 [64], P('users'), may hold values from 0.3 to 1.5
- noise_floor: float32 [64], replicated, may hold values from 0.05 to 0.5
Outputs:
- precoders: bfloat16 [64, 32, 16, 128], P('users', 'rb')
- track_metric: float32 [32768, 32], P('users', 'rb')
- entry_rate: float32 [64, 32, 16], P('users', 'rb')
Inputs may be any that keep to these rules, and one draw needn't show every extreme that they name: `serving`: each aligned block of 1024 tracks holds exactly 16 tracks served by each cell. `interferers`: A track's 2 interfering cells differ from each other and from its serving cell; each aligned block of 1024 tracks holds exactly 16 tracks with a given cell in a given column. `plan`: each entry names a track served by that cell, and the 16 tracks of a cell on one resource block differ. Take a cell group g (cells g * 2 to g * 2 + 1) and an aligned block of 4 resource blocks: at most 8 of its entries name tracks of one aligned block of 1024 tracks.
All inputs are finite; a program needn't handle non-finite values.
Results may differ from a plain program's by a relative error of at most 0.0035.
Values may be sent and summed in bfloat16 or wider, within the bound.
No kernel may reach another device: no remote copies, remote signals or barrier semaphores. Data moves between devices by JAX's collectives and lax.ppermute only.
A program may use at most 64 MiB of HBM per device.

v0:
```python
import jax
import jax.numpy as jnp
from jax import lax
from jax.sharding import PartitionSpec as P

ITERS = 12
HIGH = lax.Precision.HIGHEST


def real_form(beam_rows):
    antennas = beam_rows.shape[-1] // 2
    turned = jnp.concatenate([beam_rows[..., antennas:], -beam_rows[..., :antennas]], axis=-1)
    return jnp.concatenate([beam_rows, turned], axis=-2)


def embed_rows(channel_rows):
    antennas = channel_rows.shape[-1] // 2
    bottom_rows = jnp.concatenate(
        [-channel_rows[..., antennas:], channel_rows[..., :antennas]], axis=-1
    )
    return jnp.concatenate([channel_rows, bottom_rows], axis=-2)


def unscaled_beams(sched_rows, regularizer):
    beam_count = sched_rows.shape[-2]
    embedded = embed_rows(sched_rows)
    gram = jnp.einsum("crkd,crjd->crkj", embedded, embedded, preferred_element_type=jnp.float32)
    identity = jnp.eye(2 * beam_count, dtype=jnp.float32)
    gram = gram + regularizer[:, None, None, None] * identity
    gram_trace = jnp.trace(gram, axis1=2, axis2=3)
    start_inverse = (2.0 / gram_trace)[:, :, None, None] * identity

    def newton_step(iteration, inverse):
        product = jnp.einsum("crkj,crjl->crkl", gram, inverse, precision=HIGH)
        return 2.0 * inverse - jnp.einsum("crkj,crjl->crkl", inverse, product, precision=HIGH)

    inverse = lax.fori_loop(0, ITERS, newton_step, start_inverse)
    return jnp.einsum(
        "crkd,crkj->crjd", embedded.astype(jnp.float32), inverse[..., :beam_count], precision=HIGH
    )


def plain_regroup(channel, send_track, send_block, my_source, my_rank, groups, capacity):
    outgoing = channel[send_track, send_block, 0].reshape(groups, capacity, channel.shape[-1])
    arrived = lax.all_to_all(outgoing, "users", split_axis=0, concat_axis=0, tiled=True)
    return arrived[my_source, my_rank]


def return_denominators(denominator, send_track, send_block, my_source, my_rank, groups, capacity):
    outgoing = denominator[send_track, send_block].reshape(groups, capacity)
    arrived = lax.all_to_all(outgoing, "users", split_axis=0, concat_axis=0, tiled=True)
    return arrived[my_source, my_rank]


def track_fold(totals, grouped_rows, piece_forms, first_cell):
    piece_cells = piece_forms.shape[0]
    rows = lax.dynamic_slice_in_dim(grouped_rows, first_cell, piece_cells, axis=1)
    projected = jnp.einsum(
        "scqrd,crkd->scqrk", rows, piece_forms, preferred_element_type=jnp.float32
    )
    energy = jnp.sum(projected * projected, axis=-1)
    current = lax.dynamic_slice_in_dim(totals, first_cell, piece_cells, axis=1)
    return lax.dynamic_update_slice_in_dim(totals, current + energy, first_cell, axis=1)


def on_device(channel, serving, interferers, plan, regularizer, noise_floor):
    track_dev, rb_dev, slot_count, row_width = channel.shape
    cell_count = plan.shape[0]
    beam_count = plan.shape[2]
    cell_dev = regularizer.shape[0]
    served = track_dev // cell_count
    groups = lax.axis_size("users")
    my_group = lax.axis_index("users")
    entries = cell_dev * rb_dev * beam_count
    capacity = 2 * entries // groups
    rb_total = rb_dev * lax.axis_size("rb")
    all_entries = plan.reshape(groups, entries)
    owned_entry = all_entries // track_dev == my_group
    position = jnp.cumsum(owned_entry.astype(jnp.int32), axis=1) - 1
    position = jnp.where(owned_entry, position, capacity)
    entry_order = lax.broadcasted_iota(jnp.int32, (groups, entries), 1)
    local_track = all_entries - my_group * track_dev
    entry_block = entry_order // beam_count % rb_dev
    slot_iota = jnp.arange(capacity, dtype=jnp.int32)
    slot_match = (position[:, None, :] == slot_iota[None, :, None]).astype(jnp.int32)
    send_track = jnp.sum(slot_match * local_track[:, None, :], axis=2).reshape(-1)
    send_block = jnp.sum(slot_match * entry_block[:, None, :], axis=2).reshape(-1)
    my_entries = lax.dynamic_slice_in_dim(all_entries, my_group, 1, axis=0)[0]
    my_source = my_entries // track_dev
    source_match = (my_source[:, None] == jnp.arange(groups, dtype=jnp.int32)[None, :]).astype(
        jnp.int32
    )
    my_rank = jnp.sum((jnp.cumsum(source_match, axis=0) - 1) * source_match, axis=1)
    sched_rows = plain_regroup(
        channel, send_track, send_block, my_source, my_rank, groups, capacity
    )
    sched_rows = sched_rows.reshape(cell_dev, rb_dev, beam_count, row_width)
    vectors = unscaled_beams(sched_rows, regularizer)
    cell_power = lax.psum(jnp.sum(vectors * vectors, axis=(1, 2, 3)), "rb")
    precoders = (vectors * lax.rsqrt(cell_power / rb_total + 1e-06)[:, None, None, None]).astype(
        jnp.bfloat16
    )
    own_forms = real_form(precoders)
    heard_cells = jnp.concatenate([serving[:, None], interferers], axis=1)
    track_iota = jnp.arange(track_dev, dtype=jnp.int32)
    slot_cells = heard_cells.T
    orders = jnp.argsort(slot_cells * track_dev + track_iota[None, :], axis=1)
    ranks = jnp.argsort(orders, axis=1)
    grouped = jnp.stack(
        [channel[orders[slot_number], :, slot_number] for slot_number in range(slot_count)]
    )
    grouped_rows = grouped.reshape(slot_count, cell_count, served, rb_dev, row_width)
    zero_powers = jnp.zeros((slot_count, cell_count, served, rb_dev), jnp.float32)
    grouped_power = track_fold(
        zero_powers,
        grouped_rows,
        real_form(lax.all_gather(precoders, "users", axis=0, tiled=True)),
        jnp.int32(0),
    )
    grouped_power = grouped_power.reshape(slot_count, track_dev, rb_dev)
    track_power = jnp.stack(
        [grouped_power[slot_number][ranks[slot_number]] for slot_number in range(slot_count)],
        axis=2,
    )
    interference = track_power[:, :, 1]
    slot_number = 2
    interference = interference + track_power[:, :, slot_number]
    floor_match = (serving[:, None] == jnp.arange(cell_count, dtype=jnp.int32)[None, :]).astype(
        jnp.float32
    )
    track_floor = jnp.sum(floor_match * noise_floor[None, :], axis=1)
    denominator = interference + track_floor[:, None]
    track_metric = jnp.log2(1.0 + track_power[:, :, 0] / denominator)
    entry_denominator = return_denominators(
        denominator, send_track, send_block, my_source, my_rank, groups, capacity
    )
    crossed = jnp.einsum(
        "crkd,crjd->crkj", sched_rows, own_forms, preferred_element_type=jnp.float32
    )
    magnitude = (
        crossed[..., :beam_count] * crossed[..., :beam_count]
        + crossed[..., beam_count:] * crossed[..., beam_count:]
    )
    identity = jnp.eye(beam_count, dtype=jnp.float32)
    signal = jnp.sum(magnitude * identity, axis=-1)
    leakage = jnp.sum(magnitude * (1.0 - identity), axis=-1)
    entry_rate = jnp.log2(
        1.0 + signal / (leakage + entry_denominator.reshape(cell_dev, rb_dev, beam_count))
    )
    return (precoders, track_metric, entry_rate)


def solution(mesh):
    return jax.shard_map(
        on_device,
        mesh=mesh,
        in_specs=(
            P("users", "rb", None, None),
            P("users"),
            P("users", None),
            P(None, "rb", None),
            P("users"),
            P(),
        ),
        out_specs=(P("users", "rb", None, None), P("users", "rb"), P("users", "rb", None)),
        check_vma=False,
    )
```

profile of v0, /device:TPU:16, one launch (start us, length us, event | category | flops | bytes accessed | tf_op | source)
XLA Modules:
  0.0 197.5 jit_solution(13397811809178925806)
XLA Ops:
  8.0 1.0 copy.51
  9.5 1.2 select_reduce_fusion.2
  10.9 2.5 %gather_fusion = bf16[256,128]{1,0:T(8,128)(2,1)} fusion(bf16[1024,4,3,128]{3,1,2,0:T(4,128)(2,1)S(1)} %copy-done, s32[256]{0:T(256)S(1)} %bitcast.88), kind=kCustom, calls=%fused_computation | custom fusion | bytes 134144 | tf_op jit(solution)/shard_map/gather | solution.py:44
  13.4 11.3 %all-to-all-start = ((bf16[32,8,128]{2,1,0:T(8,128)(2,1)}), bf16[32,8,128]{2,1,0:T(8,128)(2,1)S(1)}, u32[]{:S(2)}, u32[]{:S(2)}) async-start(bf16[32,8,128]{2,1,0:T(8,128)(2,1)} %bitcast.2), calls=%async_computation | async-start | bytes 131072 | tf_op jit(solution)/shard_map/all_to_all | solution.py:45
  24.8 1.3 fusion.24
  28.1 7.0 %sort.34.cloned.1.call-done = (s32[3,1024]{1,0:T(4,128)}, s32[3,1024]{1,0:T(4,128)}) async-done(((s32[3,1024]{1,0:T(4,128)}, s32[3,1024]{1,0:T(4,128)}), (s32[3,1024]{1,0:T(4,128)}, s32[3,1024]{1,0:T(4,128)})) %sort.34.cloned.1.call-update) | async-done | bytes 24592 | tf_op jit(solution)/shard_map/jit(argsort)/sort | solution.py:107
  35.8 1.1 gather_fusion.1
  37.4 7.6 %while.10 = (s32[]{:T(128)}, f32[2,4,32,32]{2,3,1,0:T(8,128)S(1)}, f32[2,4,32,32]{3,2,1,0:T(8,128)S(1)}, s32[]{:T(128)}) while((s32[]{:T(128)}, f32[2,4,32,32]{2,3,1,0:T(8,128)S(1)}, f32[2,4,32,32]{3,2,1,0:T(8,128)S(1)}, s32[]{:T(128)}) %tuple.44), condition=%wide.region_7.8_spmd, body=%wide.region_6.7_spmd.sunk | while | flops 6307842 | bytes 262197 | solution.py:37
  45.4 10.1 %psum.7 = f32[2]{0:T(128)S(1)} all-reduce(f32[2]{0:T(128)S(1)} %get-tuple-element.71), channel_id=1, replica_groups=mesh['users'=32,'rb'=8] {'rb'}, use_global_device_ids=true, to_apply=%region_9.10 | all-reduce | flops 2 | bytes 16 | tf_op jit(solution)/shard_map/psum | solution.py:99
  57.8 8.9 %gather_fusion.3 = bf16[1024,4,128]{2,1,0:T(4,128)(2,1)} fusion(bf16[1024,4,3,128]{3,1,2,0:T(4,128)(2,1)S(1)} %copy-done, s32[1024]{0:T(1024)S(1)} %bitcast.87), kind=kCustom, calls=%fused_computation.3 | custom fusion | bytes 2105344 | tf_op jit(solution)/shard_map/gather | solution.py:110
  66.6 2.5 %copy.57 = bf16[1,64,16,4,128]{4,2,0,3,1:T(8,128)(2,1)} copy(bf16[1,64,16,4,128]{4,3,2,1,0:T(4,128)(2,1)} %bitcast.94) | data formatting | bytes 2097152 | tf_op jit(solution)/shard_map/stack | solution.py:109
  69.2 8.9 %gather_fusion.4 = bf16[1024,4,128]{2,1,0:T(4,128)(2,1)} fusion(bf16[1024,4,3,128]{3,1,2,0:T(4,128)(2,1)S(1)} %copy-done, s32[1024]{0:T(1024)S(1)} %bitcast.86), kind=kCustom, calls=%fused_computation.4 | custom fusion | bytes 2105344 | tf_op jit(solution)/shard_map/gather | solution.py:110
  78.0 2.5 %copy.58 = bf16[1,64,16,4,128]{4,2,0,3,1:T(8,128)(2,1)} copy(bf16[1,64,16,4,128]{4,3,2,1,0:T(4,128)(2,1)} %bitcast.95) | data formatting | bytes 2097152 | tf_op jit(solution)/shard_map/stack | solution.py:109
  80.5 8.9 %gather_fusion.2 = bf16[1024,4,128]{2,1,0:T(4,128)(2,1)} fusion(bf16[1024,4,3,128]{3,1,2,0:T(4,128)(2,1)S(1)} %copy-done, s32[1024]{0:T(1024)S(1)} %bitcast.85), kind=kCustom, calls=%fused_computation.2 | custom fusion | bytes 2105344 | tf_op jit(solution)/shard_map/gather | solution.py:110
  89.4 2.5 %copy.56 = bf16[1,64,16,4,128]{4,2,0,3,1:T(8,128)(2,1)} copy(bf16[1,64,16,4,128]{4,3,2,1,0:T(4,128)(2,1)} %bitcast.96) | data formatting | bytes 2097152 | tf_op jit(solution)/shard_map/stack | solution.py:109
  91.8 0.8 compare_select_fusion
  93.0 42.4 %all-gather.2.cloned.1.call-done = bf16[64,4,16,128]{3,2,1,0:T(8,128)(2,1)} async-done(((bf16[2,4,16,128]{3,2,1,0:T(8,128)(2,1)}), bf16[64,4,16,128]{3,2,1,0:T(8,128)(2,1)}) %all-gather.2.cloned.1.call-update) | async-done | bytes 1048592 | tf_op jit(solution)/shard_map/all_gather | solution.py:117
  135.4 2.1 %fusion.53 = (bf16[64,4,16,64]{3,2,1,0:T(8,128)(2,1)S(1)}, bf16[64,4,16,64]{3,2,1,0:T(8,128)(2,1)S(1)}) fusion(bf16[64,4,16,128]{3,2,1,0:T(8,128)(2,1)} %all-gather.2.cloned.1.call-done), kind=kLoop, calls=%fused_computation.137 | loop fusion | flops 262144 | bytes 2097152 | tf_op jit(solution)/shard_map/slice | solution.py:12
  138.2 2.7 %multiply_reduce_fusion = f32[64,4,3,16]{3,2,1,0:T(4,128)S(1)} fusion(bf16[1,64,16,4,128]{4,2,0,3,1:T(8,128)(2,1)S(1)} %copy-done.3, bf16[1,64,16,4,128]{4,2,0,3,1:T(8,128)(2,1)S(1)} %copy-done.2, bf16[1,64,16,4,128]{4,2,0,3,1:T(8,128)(2,1)S(1)} %copy-done.4, bf16[64,4,16,64]{3,2,1,0:T(8,128)(2,1)S(1)} %get-tuple-element.55, ...), kind=kOutput, calls=%fused_computation.12 | convolution fusion | flops 117166080 | bytes 5292032 | tf_op jit(solution)/shard_map/scqrd,crkd->scqrk/dot_general | solution.py:58
  141.0 0.9 fusion.54
  141.9 2.2 %copy.61 = f32[1,64,16,4]{3,2,1,0:T(8,128)} copy(f32[1,64,16,4]{2,0,3,1:T(1,128)} %get-tuple-element.56) | data formatting | bytes 32768 | tf_op jit(solution)/shard_map/slice | solution.py:122
  144.0 1.3 copy.60
  145.3 1.3 copy.59
  146.5 5.0 %gather_fusion.7 = f32[1024,4]{1,0:T(8,128)} fusion(f32[1024,4]{1,0:T(8,128)} %bitcast.92, s32[1024]{0:T(1024)S(1)} %broadcast_clamp_fusion), kind=kCustom, calls=%fused_computation.7 | custom fusion | bytes 36864 | tf_op jit(solution)/shard_map/gather | solution.py:122
  151.6 5.0 %gather_fusion.6 = f32[1024,4]{1,0:T(8,128)} fusion(f32[1024,4]{1,0:T(8,128)} %bitcast.90, s32[1024]{0:T(1024)S(1)} %broadcast_clamp_fusion.1), kind=kCustom, calls=%fused_computation.6 | custom fusion | bytes 36864 | tf_op jit(solution)/shard_map/gather | solution.py:122
  156.6 5.0 %gather_fusion.5 = f32[1024,4]{1,0:T(8,128)} fusion(f32[1024,4]{1,0:T(8,128)} %bitcast.91, s32[1024]{0:T(1024)S(1)} %broadcast_clamp_fusion.2), kind=kCustom, calls=%fused_computation.5 | custom fusion | bytes 36864 | tf_op jit(solution)/shard_map/gather | solution.py:122
  161.6 2.6 %log_multiply_fusion = (f32[1024,4]{1,0:T(8,128)}, f32[1024,4]{1,0:T(8,128)}) fusion(f32[1024,4]{1,0:T(8,128)} %gather_fusion.5, f32[1024]{0:T(1024)S(1)} %select_reduce_fusion, f32[1024,4]{1,0:T(8,128)} %gather_fusion.6, f32[1024,4]{1,0:T(8,128)} %gather_fusion.7), kind=kLoop, calls=%fused_computation.25 | loop fusion | flops 20480 | bytes 86016 | tf_op jit(solution)/shard_map/log2 | solution.py:133
  164.2 5.6 %gather_fusion.8 = f32[256]{0:T(256)S(1)} fusion(f32[1024,4]{1,0:T(8,128)} %get-tuple-element.51, s32[256]{0:T(256)S(1)} %bitcast.89), kind=kCustom, calls=%fused_computation.8 | custom fusion | bytes 4096 | tf_op jit(solution)/shard_map/gather | solution.py:50
  170.5 7.8 %all-to-all-start.1 = ((f32[32,1,8]{2,1,0:T(1,128)}), f32[32,1,8]{2,1,0:T(1,128)S(1)}, u32[]{:S(2)}, u32[]{:S(2)}) async-start(f32[32,1,8]{2,1,0:T(1,128)} %bitcast.31), calls=%async_computation.1 | async-start | bytes 32768 | tf_op jit(solution)/shard_map/all_to_all | solution.py:51
  178.5 1.8 copy.63
  180.4 7.8 %all-to-all-done.1 = f32[32,1,8]{2,1,0:T(1,128)S(1)} async-done(((f32[32,1,8]{2,1,0:T(1,128)}), f32[32,1,8]{2,1,0:T(1,128)S(1)}, u32[]{:S(2)}, u32[]{:S(2)}) %all-to-all-start.1) | async-done | bytes 1056 | tf_op jit(solution)/shard_map/all_to_all | solution.py:51
  188.1 1.3 gather_fusion.9
  (101 shorter events, 16.1 us)
Async XLA Ops:
  8.0 2.9 %copy-start = (bf16[1024,4,3,128]{3,1,2,0:T(4,128)(2,1)S(1)}, bf16[1024,4,3,128]{3,1,2,0:T(4,128)(2,1)}, u32[]{:S(2)}) copy-start(bf16[1024,4,3,128]{3,1,2,0:T(4,128)(2,1)} %param.8) | copy-start | bytes 9437188
  13.4 22.4 %all-to-all-start = ((bf16[32,8,128]{2,1,0:T(8,128)(2,1)}), bf16[32,8,128]{2,1,0:T(8,128)(2,1)S(1)}, u32[]{:S(2)}, u32[]{:S(2)}) async-start(bf16[32,8,128]{2,1,0:T(8,128)(2,1)} %bitcast.2), calls=%async_computation | async-start | bytes 131072 | tf_op jit(solution)/shard_map/all_to_all | solution.py:45
  24.8 10.4 %sort.34.cloned.1.call-start = ((), (), s32[]{:S(2)}) async-start(), calls=%async_computation.3 | async-start | bytes 98336 | tf_op jit(solution)/shard_map/jit(argsort)/sort | solution.py:107
  26.8 65.1 %sort.36.cloned.1.call-start = ((), (), s32[]{:S(2)}) async-start(), calls=%async_computation.4 | async-start | bytes 98336 | tf_op jit(solution)/shard_map/jit(argsort)/sort | solution.py:108
  35.8 99.7 %all-gather.2.cloned.1.call-start = ((), (), s32[]{:S(2)}) async-start(), calls=%async_computation.2 | async-start | bytes 1081344 | tf_op jit(solution)/shard_map/all_gather | solution.py:117
  37.0 20.7 %copy-start.6 = (s32[3,1024]{1,0:T(4,128)S(1)}, s32[3,1024]{1,0:T(4,128)}, u32[]{:S(2)}) copy-start(s32[3,1024]{1,0:T(4,128)} %get-tuple-element.23) | copy-start | bytes 36868
  78.0 14.7 %copy-start.5 = (bf16[2,4,16,128]{3,2,1,0:T(8,128)(2,1)S(1)}, bf16[2,4,16,128]{3,2,1,0:T(8,128)(2,1)}, u32[]{:S(2)}) copy-start(bf16[2,4,16,128]{3,2,1,0:T(8,128)(2,1)} %multiply_convert_fusion) | copy-start | bytes 98308
  135.4 2.1 %copy-start.1 = (bf16[64,4,16,128]{3,2,1,0:T(8,128)(2,1)S(1)}, bf16[64,4,16,128]{3,2,1,0:T(8,128)(2,1)}, u32[]{:S(2)}) copy-start(bf16[64,4,16,128]{3,2,1,0:T(8,128)(2,1)} %all-gather.2.cloned.1.call-done) | copy-start | bytes 3145732
  135.4 2.2 %copy-start.2 = (bf16[1,64,16,4,128]{4,2,0,3,1:T(8,128)(2,1)S(1)}, bf16[1,64,16,4,128]{4,2,0,3,1:T(8,128)(2,1)}, u32[]{:S(2)}) copy-start(bf16[1,64,16,4,128]{4,2,0,3,1:T(8,128)(2,1)} %copy.57) | copy-start | bytes 3145732
  135.4 2.5 %copy-start.3 = (bf16[1,64,16,4,128]{4,2,0,3,1:T(8,128)(2,1)S(1)}, bf16[1,64,16,4,128]{4,2,0,3,1:T(8,128)(2,1)}, u32[]{:S(2)}) copy-start(bf16[1,64,16,4,128]{4,2,0,3,1:T(8,128)(2,1)} %copy.58) | copy-start | bytes 3145732
  135.4 2.8 %copy-start.4 = (bf16[1,64,16,4,128]{4,2,0,3,1:T(8,128)(2,1)S(1)}, bf16[1,64,16,4,128]{4,2,0,3,1:T(8,128)(2,1)}, u32[]{:S(2)}) copy-start(bf16[1,64,16,4,128]{4,2,0,3,1:T(8,128)(2,1)} %copy.56) | copy-start | bytes 3145732
  156.6 21.7 %copy-start.7 = (f32[16,16]{1,0:T(8,128)S(1)}, f32[16,16]{1,0:T(8,128)}, u32[]{:S(2)}) copy-start(f32[16,16]{1,0:T(8,128)} %fusion.26) | copy-start | bytes 3076
  170.5 17.7 %all-to-all-start.1 = ((f32[32,1,8]{2,1,0:T(1,128)}), f32[32,1,8]{2,1,0:T(1,128)S(1)}, u32[]{:S(2)}, u32[]{:S(2)}) async-start(f32[32,1,8]{2,1,0:T(1,128)} %bitcast.31), calls=%async_computation.1 | async-start | bytes 32768 | tf_op jit(solution)/shard_map/all_to_all | solution.py:51
Sparse Core Ops, SparseCore 0:
  28.6 6.2 sort.38.cloned.1.call-done
  38.2 4.3 sort.40.cloned.1.call-done
  (2 shorter events, 0.0 us)
Sparse Core Ops, SparseCore 1:
  56.4 79.0 all-gather.1
where the time goes:
time: 199 us; the launch traced here: 198 us
  local copies, waits for them, and re-layouts  78.3 us (39%)
  waiting for transfers between devices  50.2 us (25%)
  starting transfers between devices  19.2 us (10%)
  between operations  15.8 us (8%)
  other arithmetic  12.8 us (6%)
  matrix products  10.6 us (5%)
  blocking collectives  10.1 us (5%)
    all_gather x1, waiting for transfers between devices, on_device(): lax.all_gather(precoders, 'users', axis=0, tiled=True)  42.4 us
    gather x3, local copies, waits for them, and re-layouts, on_device(): channel[orders[slot_number], :, slot_number]  26.6 us
    gather x3, local copies, waits for them, and re-layouts, on_device(): grouped_power[slot_number][ranks[slot_number]]  15.1 us
    all_to_all x1, starting transfers between devices, plain_regroup(): lax.all_to_all(outgoing, 'users', split_axis=0, concat_axis=0, tiled=True)  11.3 us
    psum x1, blocking collectives, on_device(): cell_power = lax.psum(jnp.sum(vectors * vectors, axis=(1, 2, 3)), 'rb')  10.1 us
    all_to_all x1, starting transfers between devices, return_denominators(): lax.all_to_all(outgoing, 'users', split_axis=0, concat_axis=0, tiled=True)  7.84 us
    all_to_all x1, waiting for transfers between devices, return_denominators(): lax.all_to_all(outgoing, 'users', split_axis=0, concat_axis=0, tiled=True)  7.76 us
    another operation x3, local copies, waits for them, and re-layouts, on_device(): jnp.stack([channel[orders[slot_number], :, slot_number] for slot_number i...  7.47 us
  transfers between devices with their start and end apart: 3, of which 2 were waited for; matrix products, arithmetic and copies ran while one was open for 22% of the time, Pallas kernels for 0%

commit v1 on v0

--- a/solution.py
+++ b/solution.py
@@ -114,7 +114,12 @@
     grouped_power = track_fold(
         zero_powers,
         grouped_rows,
-        real_form(lax.all_gather(precoders, "users", axis=0, tiled=True)),
+        real_form(
+            jnp.concatenate(
+                lax.all_to_all(jnp.stack([precoders] * lax.axis_size("users")), "users", 0, 0),
+                axis=0,
+            )
+        ),
         jnp.int32(0),
     )
     grouped_power = grouped_power.reshape(slot_count, track_dev, rb_dev)

time: 199 us -> 175 us (0.88)
  waiting for transfers between devices: 50.2 us -> 16.5 us
  starting transfers between devices: 19.2 us -> 26.6 us
  local copies, waits for them, and re-layouts: 78.3 us -> 81.1 us
    all_gather x1 -> x0, waiting for transfers between devices: 42.4 us -> none  [on_device(): lax.all_gather(precoders, 'users', axis=0, tiled=True)]
    all_to_all x1, waiting for transfers between devices: 0.01 us -> 8.7 us  [plain_regroup(): lax.all_to_all(outgoing, 'users', split_axis=0, concat_axis=0, tiled=True)]
    all_to_all x0 -> x1, starting transfers between devices: none -> 4.66 us  [on_device(): lax.all_to_all(jnp.stack([precoders] * lax.axis_size('users')), 'users',...]
    all_to_all x1, starting transfers between devices: 7.84 us -> 10.7 us  [return_denominators(): lax.all_to_all(outgoing, 'users', split_axis=0, concat_axis=0, tiled=True)]
  transfers between devices with their start and end apart: 3 -> 3, of which waited for: 2 -> 2; matrix products, arithmetic and copies ran while one was open for 22% -> 24% of each run, Pallas kernels for 0% -> 0%
where the time goes in v1:
time: 175 us; the launch traced here: 172 us
  local copies, waits for them, and re-layouts  81.1 us (46%)
  starting transfers between devices  26.6 us (15%)
  waiting for transfers between devices  16.5 us (9%)
  between operations  14.4 us (8%)
  matrix products  11.4 us (7%)
  other arithmetic  11 us (6%)
  blocking collectives  10.4 us (6%)
    gather x3, local copies, waits for them, and re-layouts, on_device(): channel[orders[slot_number], :, slot_number]  26.6 us
    gather x3, local copies, waits for them, and re-layouts, on_device(): grouped_power[slot_number][ranks[slot_number]]  15.1 us
    all_to_all x1, starting transfers between devices, plain_regroup(): lax.all_to_all(outgoing, 'users', split_axis=0, concat_axis=0, tiled=True)  11.3 us
    all_to_all x1, starting transfers between devices, return_denominators(): lax.all_to_all(outgoing, 'users', split_axis=0, concat_axis=0, tiled=True)  10.7 us
    psum x1, blocking collectives, on_device(): cell_power = lax.psum(jnp.sum(vectors * vectors, axis=(1, 2, 3)), 'rb')  10.4 us
    sort x2, local copies, waits for them, and re-layouts, on_device(): orders = jnp.argsort(slot_cells * track_dev + track_iota[None, :], axis=1)  8.7 us
    all_to_all x1, waiting for transfers between devices, plain_regroup(): lax.all_to_all(outgoing, 'users', split_axis=0, concat_axis=0, tiled=True)  8.7 us
    all_to_all x1, waiting for transfers between devices, return_denominators(): lax.all_to_all(outgoing, 'users', split_axis=0, concat_axis=0, tiled=True)  7.78 us
  transfers between devices with their start and end apart: 3, of which 2 were waited for; matrix products, arithmetic and copies ran while one was open for 24% of the time, Pallas kernels for 0%

profile of v1, /device:TPU:16, one launch (start us, length us, event | category | flops | bytes accessed | tf_op | source)
XLA Modules:
  0.0 171.9 jit_solution(500374873413706323)
XLA Ops:
  7.2 1.0 copy.51
  8.7 1.2 select_reduce_fusion.2
  10.1 2.5 %gather_fusion = bf16[256,128]{1,0:T(8,128)(2,1)} fusion(bf16[1024,4,3,128]{3,1,2,0:T(4,128)(2,1)S(1)} %copy-done, s32[256]{0:T(256)S(1)} %bitcast.89), kind=kCustom, calls=%fused_computation | custom fusion | bytes 134144 | tf_op jit(solution)/shard_map/gather | solution.py:44
  12.6 11.3 %all-to-all-start = ((bf16[32,8,128]{2,1,0:T(8,128)(2,1)}), bf16[32,8,128]{2,1,0:T(8,128)(2,1)S(1)}, u32[]{:S(2)}, u32[]{:S(2)}) async-start(bf16[32,8,128]{2,1,0:T(8,128)(2,1)} %bitcast.2), calls=%async_computation | async-start | bytes 131072 | tf_op jit(solution)/shard_map/all_to_all | solution.py:45
  25.2 8.7 %all-to-all-done = bf16[32,8,128]{2,1,0:T(8,128)(2,1)S(1)} async-done(((bf16[32,8,128]{2,1,0:T(8,128)(2,1)}), bf16[32,8,128]{2,1,0:T(8,128)(2,1)S(1)}, u32[]{:S(2)}, u32[]{:S(2)}) %all-to-all-start) | async-done | bytes 65568 | tf_op jit(solution)/shard_map/all_to_all | solution.py:45
  33.9 1.1 gather_fusion.1
  35.6 7.6 %while.10 = (s32[]{:T(128)}, f32[2,4,32,32]{2,3,1,0:T(8,128)S(1)}, f32[2,4,32,32]{3,2,1,0:T(8,128)S(1)}, s32[]{:T(128)}) while((s32[]{:T(128)}, f32[2,4,32,32]{2,3,1,0:T(8,128)S(1)}, f32[2,4,32,32]{3,2,1,0:T(8,128)S(1)}, s32[]{:T(128)}) %tuple.44), condition=%wide.region_7.8_spmd, body=%wide.region_6.7_spmd.sunk | while | flops 6307842 | bytes 262197 | solution.py:37
  43.6 10.4 %psum.7 = f32[2]{0:T(128)S(1)} all-reduce(f32[2]{0:T(128)S(1)} %get-tuple-element.71), channel_id=1, replica_groups=mesh['users'=32,'rb'=8] {'rb'}, use_global_device_ids=true, to_apply=%region_9.10 | all-reduce | flops 2 | bytes 16 | tf_op jit(solution)/shard_map/psum | solution.py:99
  54.1 1.3 stack.10
  55.4 4.7 %all-to-all-start.1 = ((bf16[32,2,4,16,128]{4,3,2,1,0:T(8,128)(2,1)}), bf16[32,2,4,16,128]{4,3,2,1,0:T(8,128)(2,1)}, u32[]{:S(2)}, u32[]{:S(2)}) async-start(bf16[32,2,4,16,128]{4,3,2,1,0:T(8,128)(2,1)} %stack.10), calls=%async_computation.1 | async-start | bytes 2097152 | tf_op jit(solution)/shard_map/all_to_all | solution.py:119
  61.7 8.7 %sort.34.cloned.1.call-done = (s32[3,1024]{1,0:T(4,128)}, s32[3,1024]{1,0:T(4,128)}) async-done(((s32[3,1024]{1,0:T(4,128)}, s32[3,1024]{1,0:T(4,128)}), (s32[3,1024]{1,0:T(4,128)}, s32[3,1024]{1,0:T(4,128)})) %sort.34.cloned.1.call-update) | async-done | bytes 24592 | tf_op jit(solution)/shard_map/jit(argsort)/sort | solution.py:107
  71.9 8.9 %gather_fusion.3 = bf16[1024,4,128]{2,1,0:T(4,128)(2,1)} fusion(bf16[1024,4,3,128]{3,1,2,0:T(4,128)(2,1)S(1)} %copy-done, s32[1024]{0:T(1024)S(1)} %bitcast.88), kind=kCustom, calls=%fused_computation.3 | custom fusion | bytes 2105344 | tf_op jit(solution)/shard_map/gather | solution.py:110
  80.8 2.5 %copy.57 = bf16[1,64,16,4,128]{4,2,0,3,1:T(8,128)(2,1)} copy(bf16[1,64,16,4,128]{4,3,2,1,0:T(4,128)(2,1)} %bitcast.95) | data formatting | bytes 2097152 | tf_op jit(solution)/shard_map/stack | solution.py:109
  83.2 8.9 %gather_fusion.4 = bf16[1024,4,128]{2,1,0:T(4,128)(2,1)} fusion(bf16[1024,4,3,128]{3,1,2,0:T(4,128)(2,1)S(1)} %copy-done, s32[1024]{0:T(1024)S(1)} %bitcast.87), kind=kCustom, calls=%fused_computation.4 | custom fusion | bytes 2105344 | tf_op jit(solution)/shard_map/gather | solution.py:110
  92.1 2.5 %copy.58 = bf16[1,64,16,4,128]{4,2,0,3,1:T(8,128)(2,1)} copy(bf16[1,64,16,4,128]{4,3,2,1,0:T(4,128)(2,1)} %bitcast.96) | data formatting | bytes 2097152 | tf_op jit(solution)/shard_map/stack | solution.py:109
  94.6 8.9 %gather_fusion.2 = bf16[1024,4,128]{2,1,0:T(4,128)(2,1)} fusion(bf16[1024,4,3,128]{3,1,2,0:T(4,128)(2,1)S(1)} %copy-done, s32[1024]{0:T(1024)S(1)} %bitcast.86), kind=kCustom, calls=%fused_computation.2 | custom fusion | bytes 2105344 | tf_op jit(solution)/shard_map/gather | solution.py:110
  103.5 2.5 %copy.56 = bf16[1,64,16,4,128]{4,2,0,3,1:T(8,128)(2,1)} copy(bf16[1,64,16,4,128]{4,3,2,1,0:T(4,128)(2,1)} %bitcast.97) | data formatting | bytes 2097152 | tf_op jit(solution)/shard_map/stack | solution.py:109
  107.2 2.1 %fusion.53 = (bf16[64,4,16,64]{3,2,1,0:T(8,128)(2,1)S(1)}, bf16[64,4,16,64]{3,2,1,0:T(8,128)(2,1)S(1)}) fusion(bf16[64,4,16,128]{3,2,1,0:T(8,128)(2,1)} %bitcast.8), kind=kLoop, calls=%fused_computation.137 | loop fusion | flops 262144 | bytes 2097152 | tf_op jit(solution)/shard_map/slice | solution.py:12
  109.6 3.5 %multiply_reduce_fusion = f32[64,4,3,16]{3,2,1,0:T(4,128)S(1)} fusion(bf16[1,64,16,4,128]{4,2,0,3,1:T(8,128)(2,1)S(1)} %copy-done.2, bf16[1,64,16,4,128]{4,2,0,3,1:T(8,128)(2,1)S(1)} %copy-done.1, bf16[1,64,16,4,128]{4,2,0,3,1:T(8,128)(2,1)S(1)} %copy-done.3, bf16[64,4,16,64]{3,2,1,0:T(8,128)(2,1)S(1)} %get-tuple-element.55, ...), kind=kOutput, calls=%fused_computation.12 | convolution fusion | flops 117166080 | bytes 5292032 | tf_op jit(solution)/shard_map/scqrd,crkd->scqrk/dot_general | solution.py:58
  113.1 0.9 fusion.54
  114.1 2.2 %copy.61 = f32[1,64,16,4]{3,2,1,0:T(8,128)} copy(f32[1,64,16,4]{2,0,3,1:T(1,128)} %get-tuple-element.56) | data formatting | bytes 32768 | tf_op jit(solution)/shard_map/slice | solution.py:127
  116.2 1.3 copy.60
  117.5 1.3 copy.59
  118.7 5.0 %gather_fusion.7 = f32[1024,4]{1,0:T(8,128)} fusion(f32[1024,4]{1,0:T(8,128)} %bitcast.93, s32[1024]{0:T(1024)S(1)} %broadcast_clamp_fusion), kind=kCustom, calls=%fused_computation.7 | custom fusion | bytes 36864 | tf_op jit(solution)/shard_map/gather | solution.py:127
  123.8 5.0 %gather_fusion.6 = f32[1024,4]{1,0:T(8,128)} fusion(f32[1024,4]{1,0:T(8,128)} %bitcast.91, s32[1024]{0:T(1024)S(1)} %broadcast_clamp_fusion.1), kind=kCustom, calls=%fused_computation.6 | custom fusion | bytes 36864 | tf_op jit(solution)/shard_map/gather | solution.py:127
  128.8 5.0 %gather_fusion.5 = f32[1024,4]{1,0:T(8,128)} fusion(f32[1024,4]{1,0:T(8,128)} %bitcast.92, s32[1024]{0:T(1024)S(1)} %broadcast_clamp_fusion.2), kind=kCustom, calls=%fused_computation.5 | custom fusion | bytes 36864 | tf_op jit(solution)/shard_map/gather | solution.py:127
  133.8 2.6 %log_multiply_fusion = (f32[1024,4]{1,0:T(8,128)}, f32[1024,4]{1,0:T(8,128)}) fusion(f32[1024,4]{1,0:T(8,128)} %gather_fusion.5, f32[1024]{0:T(1024)S(1)} %select_reduce_fusion, f32[1024,4]{1,0:T(8,128)} %gather_fusion.6, f32[1024,4]{1,0:T(8,128)} %gather_fusion.7), kind=kLoop, calls=%fused_computation.25 | loop fusion | flops 20480 | bytes 86016 | tf_op jit(solution)/shard_map/log2 | solution.py:138
  136.4 5.6 %gather_fusion.8 = f32[256]{0:T(256)S(1)} fusion(f32[1024,4]{1,0:T(8,128)} %get-tuple-element.51, s32[256]{0:T(256)S(1)} %bitcast.90), kind=kCustom, calls=%fused_computation.8 | custom fusion | bytes 4096 | tf_op jit(solution)/shard_map/gather | solution.py:50
  142.6 10.7 %all-to-all-start.2 = ((f32[32,1,8]{2,1,0:T(1,128)}), f32[32,1,8]{2,1,0:T(1,128)S(1)}, u32[]{:S(2)}, u32[]{:S(2)}) async-start(f32[32,1,8]{2,1,0:T(1,128)} %bitcast.32), calls=%async_computation.2 | async-start | bytes 32768 | tf_op jit(solution)/shard_map/all_to_all | solution.py:51
  153.5 1.8 %copy.63 = f32[1024,4]{0,1:T(4,128)} copy(f32[1024,4]{1,0:T(8,128)} %get-tuple-element.50) | data formatting | bytes 32768
  155.3 7.8 %all-to-all-done.2 = f32[32,1,8]{2,1,0:T(1,128)S(1)} async-done(((f32[32,1,8]{2,1,0:T(1,128)}), f32[32,1,8]{2,1,0:T(1,128)S(1)}, u32[]{:S(2)}, u32[]{:S(2)}) %all-to-all-start.2) | async-done | bytes 1056 | tf_op jit(solution)/shard_map/all_to_all | solution.py:51
  163.1 1.3 gather_fusion.9
  (101 shorter events, 16.3 us)
Async XLA Ops:
  7.2 2.9 %copy-start = (bf16[1024,4,3,128]{3,1,2,0:T(4,128)(2,1)S(1)}, bf16[1024,4,3,128]{3,1,2,0:T(4,128)(2,1)}, u32[]{:S(2)}) copy-start(bf16[1024,4,3,128]{3,1,2,0:T(4,128)(2,1)} %param.8) | copy-start | bytes 9437188
  12.6 21.3 %all-to-all-start = ((bf16[32,8,128]{2,1,0:T(8,128)(2,1)}), bf16[32,8,128]{2,1,0:T(8,128)(2,1)S(1)}, u32[]{:S(2)}, u32[]{:S(2)}) async-start(bf16[32,8,128]{2,1,0:T(8,128)(2,1)} %bitcast.2), calls=%async_computation | async-start | bytes 131072 | tf_op jit(solution)/shard_map/all_to_all | solution.py:45
  35.6 24.5 %copy-start.5 = (s32[1024]{0:T(1024)S(1)}, s32[1024]{0:T(1024)}, u32[]{:S(2)}) copy-start(s32[1024]{0:T(1024)} %param.9) | copy-start | bytes 12292
  35.6 24.5 %copy-start.6 = (s32[1024,2]{0,1:T(2,128)S(1)}, s32[1024,2]{0,1:T(2,128)}, u32[]{:S(2)}) copy-start(s32[1024,2]{0,1:T(2,128)} %param.10) | copy-start | bytes 24580
  35.6 26.0 %copy-start.7 = (f32[64]{0:T(128)S(1)}, f32[64]{0:T(128)}, u32[]{:S(2)}) copy-start(f32[64]{0:T(128)} %param.13) | copy-start | bytes 772
  54.1 52.8 %copy-start.4 = (bf16[2,4,16,128]{3,2,1,0:T(8,128)(2,1)}, bf16[2,4,16,128]{3,2,1,0:T(8,128)(2,1)S(1)}, u32[]{:S(2)}) copy-start(bf16[2,4,16,128]{3,2,1,0:T(8,128)(2,1)S(1)} %multiply_convert_fusion) | copy-start | bytes 98308
  55.4 51.8 %all-to-all-start.1 = ((bf16[32,2,4,16,128]{4,3,2,1,0:T(8,128)(2,1)}), bf16[32,2,4,16,128]{4,3,2,1,0:T(8,128)(2,1)}, u32[]{:S(2)}, u32[]{:S(2)}) async-start(bf16[32,2,4,16,128]{4,3,2,1,0:T(8,128)(2,1)} %stack.10), calls=%async_computation.1 | async-start | bytes 2097152 | tf_op jit(solution)/shard_map/all_to_all | solution.py:119
  60.0 10.4 %sort.34.cloned.1.call-start = ((), (), s32[]{:S(2)}) async-start(), calls=%async_computation.3 | async-start | bytes 98336 | tf_op jit(solution)/shard_map/jit(argsort)/sort | solution.py:107
  61.4 44.6 %sort.36.cloned.1.call-start = ((), (), s32[]{:S(2)}) async-start(), calls=%async_computation.4 | async-start | bytes 98336 | tf_op jit(solution)/shard_map/jit(argsort)/sort | solution.py:108
  107.2 2.1 %copy-start.1 = (bf16[1,64,16,4,128]{4,2,0,3,1:T(8,128)(2,1)S(1)}, bf16[1,64,16,4,128]{4,2,0,3,1:T(8,128)(2,1)}, u32[]{:S(2)}) copy-start(bf16[1,64,16,4,128]{4,2,0,3,1:T(8,128)(2,1)} %copy.57) | copy-start | bytes 3145732
  107.2 2.2 %copy-start.2 = (bf16[1,64,16,4,128]{4,2,0,3,1:T(8,128)(2,1)S(1)}, bf16[1,64,16,4,128]{4,2,0,3,1:T(8,128)(2,1)}, u32[]{:S(2)}) copy-start(bf16[1,64,16,4,128]{4,2,0,3,1:T(8,128)(2,1)} %copy.58) | copy-start | bytes 3145732
  107.2 2.5 %copy-start.3 = (bf16[1,64,16,4,128]{4,2,0,3,1:T(8,128)(2,1)S(1)}, bf16[1,64,16,4,128]{4,2,0,3,1:T(8,128)(2,1)}, u32[]{:S(2)}) copy-start(bf16[1,64,16,4,128]{4,2,0,3,1:T(8,128)(2,1)} %copy.56) | copy-start | bytes 3145732
  142.6 20.5 %all-to-all-start.2 = ((f32[32,1,8]{2,1,0:T(1,128)}), f32[32,1,8]{2,1,0:T(1,128)S(1)}, u32[]{:S(2)}, u32[]{:S(2)}) async-start(f32[32,1,8]{2,1,0:T(1,128)} %bitcast.32), calls=%async_computation.2 | async-start | bytes 32768 | tf_op jit(solution)/shard_map/all_to_all | solution.py:51
Sparse Core Ops, SparseCore 0:
  63.9 6.2 sort.38.cloned.1.call-done
  73.4 4.3 sort.40.cloned.1.call-done
  (2 shorter events, 0.0 us)
